TPU v7x, 32 devices: a whole 2x2x4 slice. The times are simulated.
32 devices in a mesh: comp: 8 (over z, y), harm: 4 (over x, core).
Axes of the slice: x: 2, y: 2, z: 4, core: 2. Of those that a mesh axis runs over, the one named last changes fastest.
Arguments:
- load: float32 [128, 32768], P('harm', 'comp'), may hold values from -6 to 6
- stiff_blocks: bfloat16 [256, 8, 128, 128], P('comp'), as said below
- mass_blocks: bfloat16 [256, 8, 128, 128], P('comp'), as said below
- block_cols: int32 [256, 8], P('comp'), may hold values from -8 to 263, as said below
- contact_rows: int32 [8, 256], P('comp'), may hold values from 0 to 4095, as said below
- partner_slot: int32 [8, 256], P('comp'), may hold values from 0 to 255, each once within a row
- contact_count: int32 [8], P('comp'), may hold values from 32 to 256, as said below
- normal_load: float32 [8, 256], P('comp'), may hold values from 0.3 to 3
- contact_stiffness: float32 [8, 256], P('comp'), may hold values from 0.3 to 3
- frequency: float32 [1], replicated, may hold values from 0.2 to 1
Outputs:
- displacement: float32 [128, 32768], P('harm', 'comp')
- residual: float32 [128, 32768], P('harm', 'comp')
Inputs may be any that keep to these rules, and one draw needn't show every extreme that they name: `block_cols`: entry 0 of block row r is r; its other 7 entries are distinct, differ from r by 1 to 8, and include r - 8 and r + 8; columns outside 0 .. 255 refer to zero parts of the field. `contact_rows`: the 256 entries of one group are distinct. Slots 0 .. contact_count[d]-1 of group d are live; the others carry no force. `stiff_blocks`: slot 0 of every block row is the block on the diagonal. `mass_blocks`: slot 0 of every block row is the block on the diagonal.
All inputs are finite; a program needn't handle non-finite values.
Results may differ from a plain program's by a relative error of at most 0.015.
The roundings to bfloat16 on the way count: a program that leaves them out, or rounds other values in their place, can miss the bound.
Values may be sent and summed in bfloat16 or wider, within the bound.
A program may use at most 64 MiB of HBM per device.

v0:
```python
import math

import jax
import jax.numpy as jnp
from jax import lax
from jax.sharding import PartitionSpec as P

H = 128
TIME_POINTS = 1024
BLK = 128
BAND = 8
ITERS = 3


def with_halo(value, sides, width):
    for axis, dim in sides:
        size, length = (lax.axis_size(axis), value.shape[dim])
        up = [(i, (i + 1) % size) for i in range(size - 1)]
        down = [(j, i) for i, j in up]
        last = lax.slice_in_dim(value, length - width, length, axis=dim)
        leading = lax.slice_in_dim(value, 0, width, axis=dim)
        before = lax.ppermute(last, axis, up)
        after = lax.ppermute(leading, axis, down)
        value = jnp.concatenate([before, value, after], axis=dim)
    return value


def swapped(block, axis, apart):
    count = lax.axis_size(axis)
    route = []
    for low in range(count):
        high = low | 1 << apart
        if high != low and high < count:
            route += [(low, high), (high, low)]
    return lax.ppermute(block, axis, route)


def harmonic_tables():
    column_list = jnp.arange(H, dtype=jnp.int32)
    harmonic_orders = jnp.where(column_list <= H // 2, column_list, column_list - H // 2)
    time_points = jnp.arange(TIME_POINTS, dtype=jnp.int32)
    phase_values = time_points[:, None] * harmonic_orders[None, :] % TIME_POINTS
    phase_angles = phase_values.astype(jnp.float32) * (2.0 * math.pi / TIME_POINTS)
    instant_table = jnp.where(
        column_list[None, :] <= H // 2, jnp.cos(phase_angles), jnp.sin(phase_angles)
    )
    weight_factors = jnp.where(column_list == 0, 1.0, 2.0).astype(jnp.float32) / TIME_POINTS
    return (instant_table, weight_factors, harmonic_orders)


def time_force(time_values, load_part, stiff_part, live_mask):
    return jnp.where(live_mask, load_part * jnp.tanh(stiff_part * time_values / load_part), 0.0)


def local(
    load,
    stiff_blocks,
    mass_blocks,
    block_cols,
    contact_rows,
    partner_slot,
    contact_count,
    normal_load,
    contact_stiffness,
    frequency,
):
    local_harm, local_dofs = load.shape
    block_rows = stiff_blocks.shape[0]
    harm_index = lax.axis_index("harm")
    first_harm = harm_index * local_harm
    first_row = lax.axis_index("comp") * block_rows
    partner_bit = lax.axis_size("comp").bit_length() - 2
    instant_table, weight_factors, harmonic_orders = harmonic_tables()
    own_waves = lax.dynamic_slice_in_dim(harmonic_orders, first_harm, local_harm)
    own_weights = lax.dynamic_slice_in_dim(weight_factors, first_harm, local_harm)
    factor = frequency[0] * own_waves.astype(jnp.float32) * (2.0 / H)
    factor = factor * factor
    stiff_diag = (
        jnp.diagonal(stiff_blocks[:, 0], axis1=1, axis2=2).astype(jnp.float32).reshape(local_dofs)
    )
    mass_diag = (
        jnp.diagonal(mass_blocks[:, 0], axis1=1, axis2=2).astype(jnp.float32).reshape(local_dofs)
    )
    dynamic = stiff_diag[None, :] - factor[:, None] * mass_diag[None, :]
    local_cols = block_cols - first_row + BAND
    slot_rows = contact_rows[0]
    slot_partner = partner_slot[0]
    slot_count = contact_count[0]
    slot_loads = normal_load[0]
    slot_stiffs = contact_stiffness[0]
    slot_ids = jnp.arange(slot_rows.shape[0], dtype=jnp.int32)
    displacement = load / dynamic
    residual = jnp.zeros_like(displacement)
    for sweep_index in range(ITERS):
        rounded = displacement.astype(jnp.bfloat16)
        gap = displacement - lax.optimization_barrier(rounded).astype(jnp.float32)
        extended = with_halo(rounded, (("comp", 1),), BAND * BLK)
        blocked = extended.reshape(local_harm, block_rows + 2 * BAND, BLK)
        picked = blocked[:, local_cols, :]
        stiff_part = jnp.einsum(
            "rsij,hrsj->hri", stiff_blocks, picked, preferred_element_type=jnp.float32
        ).reshape(local_harm, local_dofs)
        mass_part = jnp.einsum(
            "rsij,hrsj->hri", mass_blocks, picked, preferred_element_type=jnp.float32
        ).reshape(local_harm, local_dofs)
        stiff_part = stiff_part + stiff_diag[None, :] * gap
        mass_part = mass_part + mass_diag[None, :] * gap
        listed = displacement[:, slot_rows]
        mirrored = swapped(listed, "comp", partner_bit)
        relative = listed - mirrored[:, slot_partner]
        gathered = lax.all_gather(relative, "harm", axis=0, tiled=True)
        time_values = jnp.dot(instant_table, gathered, precision=lax.Precision.HIGHEST)
        live_mask = (slot_ids < slot_count)[None, :]
        forces = time_force(time_values, slot_loads[None, :], slot_stiffs[None, :], live_mask)
        own_table = lax.dynamic_slice_in_dim(instant_table, first_harm, local_harm, 1)
        own_force = (
            lax.dot_general(
                own_table, forces, (((0,), (0,)), ((), ())), precision=lax.Precision.HIGHEST
            )
            * own_weights[:, None]
        )
        residual = (
            load
            - (stiff_part - factor[:, None] * mass_part)
            - jnp.zeros_like(displacement).at[:, slot_rows].add(own_force)
        )
        displacement = displacement + residual / dynamic
    return (displacement, residual)


def solution(mesh):
    placed = (
        P("harm", "comp"),
        P("comp", None, None, None),
        P("comp", None, None, None),
        P("comp", None),
        P("comp", None),
        P("comp", None),
        P("comp"),
        P("comp", None),
        P("comp", None),
        P(),
    )
    return jax.shard_map(
        local,
        mesh=mesh,
        in_specs=placed,
        out_specs=(P("harm", "comp"), P("harm", "comp")),
        check_vma=False,
    )
```

profile of v0, /device:TPU:0, one launch (start us, length us, event | category | flops | bytes accessed | tf_op | source)
XLA Modules:
  0.0 147.2 jit_solution(12010181145722788087)
XLA Ops:
  1.4 0.5 slice-done.1
  1.9 3.3 %copy.207 = bf16[32,1,128,128]{0,3,2,1:T(8,128)(2,1)} copy(bf16[32,1,128,128]{3,2,1,0:T(8,128)(2,1)S(1)} %slice-done.1) | data formatting | bytes 2097152
  5.2 2.0 %gather_fusion = bf16[128,32]{1,0:T(8,128)(2,1)S(1)} fusion(bf16[32,128,128]{0,2,1:T(8,128)(2,1)} %bitcast.181, s32[128]{0:T(128)S(1)} %or_bitcast_fusion), kind=kCustom, calls=%fused_computation | custom fusion | bytes 17408 | tf_op jit(solution)/shard_map/jit(diagonal)/gather | solution.py:79
  7.2 3.3 %copy.208 = bf16[32,1,128,128]{0,3,2,1:T(8,128)(2,1)} copy(bf16[32,1,128,128]{3,2,1,0:T(8,128)(2,1)S(1)} %slice-done) | data formatting | bytes 2097152
  10.5 2.0 %gather_fusion.1 = bf16[128,32]{1,0:T(8,128)(2,1)S(1)} fusion(bf16[32,128,128]{0,2,1:T(8,128)(2,1)} %bitcast.180, s32[128]{0:T(128)S(1)} %or_bitcast_fusion), kind=kCustom, calls=%fused_computation.1 | custom fusion | bytes 17408 | tf_op jit(solution)/shard_map/jit(diagonal)/gather | solution.py:82
  12.7 0.2 fusion.63
  12.8 0.3 copy-done.18
  13.2 0.6 copy.183
  13.8 0.5 copy-done.28
  14.4 0.7 gather_fusion.3
  15.1 4.1 %collective-permute-start.2 = (f32[32,256]{0,1:T(8,128)S(1)}, f32[32,256]{0,1:T(8,128)S(1)}, u32[]{:S(2)}, u32[]{:S(2)}) collective-permute-start(f32[32,256]{0,1:T(8,128)S(1)} %bitcast.190), channel_id=1, source_target_pairs={{0,16},{16,0},{4,20},{20,4},{8,24},{24,8},{12,28},{28,12},{1,17},{... | collective-permute-start | bytes 98312 | tf_op jit(solution)/shard_map/ppermute | solution.py:35
  19.2 0.7 fusion.71
  19.9 3.4 %collective-permute-start = (bf16[32,1024]{1,0:T(8,128)(2,1)}, bf16[32,1024]{1,0:T(8,128)(2,1)S(1)}, u32[]{:S(2)}, u32[]{:S(2)}) collective-permute-start(bf16[32,1024]{1,0:T(8,128)(2,1)} %get-tuple-element.24), channel_id=1, source_target_pairs={{0,4},{4,8},{8,12},{12,16},{16,20},{20,24},{24,28},{1,5},{5,9},{9,... | collective-permute-start | bytes 196616 | tf_op jit(solution)/shard_map/ppermute | solution.py:22
  23.3 1.3 collective-permute-start.1
  25.3 2.7 %sine_select_fusion = f32[1024,128]{1,0:T(8,128)S(1)} fusion(s32[128]{0:T(128)} %copy-done.30, pred[128]{0:T(512)(128)(4,1)S(1)} %iota_compare_fusion.1), kind=kLoop, calls=%fused_computation.76 | loop fusion | flops 1966080 | bytes 524928 | tf_op jit(solution)/shard_map/jit(_where)/select_n | solution.py:44
  28.4 0.7 gather_fusion.4
  29.2 5.4 %all_gather.9 = f32[128,256]{1,0:T(8,128)S(1)} all-gather(f32[32,256]{1,0:T(8,128)S(1)} %copy.184), channel_id=1, replica_groups=mesh['comp'=8,'harm'=4] {'harm'}, dimensions={0}, use_global_device_ids=true | all-gather | bytes 163840 | tf_op jit(solution)/shard_map/all_gather | solution.py:111
  34.6 3.6 %fusion.11 = f32[1024,256]{1,0:T(8,128)S(1)} fusion(f32[128,256]{1,0:T(8,128)S(1)} %all_gather.9, f32[256]{0:T(256)} %bitcast.198, f32[256]{0:T(256)} %bitcast.201, pred[256]{0:T(512)(128)(4,1)S(1)} %iota_compare_fusion, s32[128]{0:T(128)} %copy-done.30, pred[128]{0:T(512)(128)(4,1)S(1)} %iota_compare_fusion.1), kind=kOutput, calls=%fused_computation.28 | convolution fusion | flops 405667840 | bytes 1182592 | tf_op jit(solution)/shard_map/dot_general | solution.py:112
  38.3 1.1 fusion.14
  39.4 0.1 copy.185
  39.5 2.2 %scatter_custom_fusion = f32[32,4096]{0,1:T(8,128)S(1)} fusion(s32[256]{0:T(256)} %bitcast.194, f32[256,32]{1,0:T(8,128)S(1)} %copy.185, f32[]{:T(128)} %constant.58.clone.1), kind=kCustom, calls=%fused_computation.45 | custom fusion | flops 8192 | bytes 524800 | tf_op jit(solution)/shard_map/scatter-add | solution.py:125
  41.8 1.4 copy.186
  43.2 0.6 copy-done.22
  43.8 1.1 copy_bitcast_fusion.2
  44.9 1.0 gather_fusion.2
  45.9 6.2 %convolution_bitcast_fusion.4 = f32[32,4,8,128]{3,2,1,0:T(8,128)S(1)} fusion(bf16[32,32,8,128]{3,0,2,1:T(8,128)(2,1)S(1)} %bitcast.176, bf16[32,8,128,128]{3,2,1,0:T(8,128)(2,1)} %param.12), kind=kOutput, calls=%fused_computation.33 | convolution fusion | flops 268435456 | bytes 11010048 | tf_op jit(solution)/shard_map/rsij,hrsj->hri/dot_general | solution.py:103
  52.1 6.2 %convolution_bitcast_fusion.5 = f32[32,4,8,128]{3,2,1,0:T(8,128)S(1)} fusion(bf16[32,32,8,128]{3,0,2,1:T(8,128)(2,1)S(1)} %bitcast.177, bf16[32,8,128,128]{3,2,1,0:T(8,128)(2,1)} %param.11), kind=kOutput, calls=%fused_computation.34 | convolution fusion | flops 268435456 | bytes 11010048 | tf_op jit(solution)/shard_map/rsij,hrsj->hri/dot_general | solution.py:100
  58.4 0.4 fusion.67
  58.8 1.9 %copy.190 = f32[32,4096]{0,1:T(8,128)} copy(f32[32,4096]{1,0:T(8,128)S(1)} %get-tuple-element.17) | data formatting | bytes 1048576 | tf_op jit(solution)/shard_map/add | solution.py:127
  60.8 2.3 %gather_fusion.6 = f32[256,32]{1,0:T(8,128)S(1)} fusion(f32[32,4096]{0,1:T(8,128)} %copy.190, s32[1024]{0:T(1024)S(1)} %pad_clamp_fusion.1), kind=kCustom, calls=%fused_computation.6 | custom fusion | bytes 66560 | tf_op jit(solution)/shard_map/gather | solution.py:108
  63.1 3.2 %collective-permute-start.5 = (f32[32,256]{0,1:T(8,128)S(1)}, f32[32,256]{0,1:T(8,128)S(1)}, u32[]{:S(2)}, u32[]{:S(2)}) collective-permute-start(f32[32,256]{0,1:T(8,128)S(1)} %bitcast.192), channel_id=1, source_target_pairs={{0,16},{16,0},{4,20},{20,4},{8,24},{24,8},{12,28},{28,12},{1,17},{... | collective-permute-start | bytes 98312 | tf_op jit(solution)/shard_map/ppermute | solution.py:35
  66.3 1.8 %collective-permute-start.3 = (bf16[32,1024]{1,0:T(8,128)(2,1)S(1)}, bf16[32,1024]{1,0:T(8,128)(2,1)S(1)}, u32[]{:S(2)}, u32[]{:S(2)}) collective-permute-start(bf16[32,1024]{1,0:T(8,128)(2,1)S(1)} %get-tuple-element.22), channel_id=1, source_target_pairs={{0,4},{4,8},{8,12},{12,16},{16,20},{20,24},{24,28},{1,5},{5,9},{9,... | collective-permute-start | bytes 196616 | tf_op jit(solution)/shard_map/ppermute | solution.py:22
  68.0 1.3 collective-permute-start.4
  69.3 3.7 %collective-permute-done.5 = f32[32,256]{0,1:T(8,128)S(1)} collective-permute-done((f32[32,256]{0,1:T(8,128)S(1)}, f32[32,256]{0,1:T(8,128)S(1)}, u32[]{:S(2)}, u32[]{:S(2)}) %collective-permute-start.5) | collective-permute-done | bytes 32800 | tf_op jit(solution)/shard_map/ppermute | solution.py:35
  73.1 0.7 gather_fusion.7
  73.9 5.4 %all_gather.10 = f32[128,256]{1,0:T(8,128)S(1)} all-gather(f32[32,256]{1,0:T(8,128)S(1)} %copy.191), channel_id=1, replica_groups=mesh['comp'=8,'harm'=4] {'harm'}, dimensions={0}, use_global_device_ids=true | all-gather | bytes 163840 | tf_op jit(solution)/shard_map/all_gather | solution.py:111
  79.3 2.9 %fusion.7 = f32[1024,256]{1,0:T(8,128)S(1)} fusion(f32[128,256]{1,0:T(8,128)S(1)} %all_gather.10, f32[256]{0:T(256)S(1)} %bitcast.199, f32[256]{0:T(256)S(1)} %bitcast.202, pred[256]{0:T(512)(128)(4,1)S(1)} %copy-done.43, s32[128]{0:T(128)S(1)} %copy-done.31, pred[128]{0:T(512)(128)(4,1)S(1)} %copy-done.36), kind=kOutput, calls=%fused_computation.23 | convolution fusion | flops 405667840 | bytes 1182592 | tf_op jit(solution)/shard_map/dot_general | solution.py:112
  82.3 1.1 fusion.13
  83.5 0.1 copy.192
  83.5 2.3 %scatter_custom_fusion.1 = f32[32,4096]{0,1:T(8,128)S(1)} fusion(s32[256]{0:T(256)} %bitcast.195, f32[256,32]{1,0:T(8,128)S(1)} %copy.192, f32[]{:T(128)} %constant.58.clone.1), kind=kCustom, calls=%fused_computation.43 | custom fusion | flops 8192 | bytes 524800 | tf_op jit(solution)/shard_map/scatter-add | solution.py:125
  85.8 1.4 copy.193
  87.2 0.6 copy-done.24
  87.9 1.1 copy_bitcast_fusion.1
  88.9 1.0 gather_fusion.5
  89.9 6.2 %convolution_bitcast_fusion.2 = f32[32,4,8,128]{3,2,1,0:T(8,128)S(1)} fusion(bf16[32,32,8,128]{3,0,2,1:T(8,128)(2,1)S(1)} %bitcast.178, bf16[32,8,128,128]{3,2,1,0:T(8,128)(2,1)} %param.12), kind=kOutput, calls=%fused_computation.31 | convolution fusion | flops 268435456 | bytes 11010048 | tf_op jit(solution)/shard_map/rsij,hrsj->hri/dot_general | solution.py:103
  96.2 6.3 %convolution_bitcast_fusion.3 = f32[32,4,8,128]{3,2,1,0:T(8,128)S(1)} fusion(bf16[32,32,8,128]{3,0,2,1:T(8,128)(2,1)S(1)} %bitcast.179, bf16[32,8,128,128]{3,2,1,0:T(8,128)(2,1)} %param.11), kind=kOutput, calls=%fused_computation.32 | convolution fusion | flops 268435456 | bytes 11010048 | tf_op jit(solution)/shard_map/rsij,hrsj->hri/dot_general | solution.py:100
  102.5 0.3 fusion.65
  102.9 1.9 %copy.197 = f32[32,4096]{0,1:T(8,128)} copy(f32[32,4096]{1,0:T(8,128)S(1)} %get-tuple-element.15) | data formatting | bytes 1048576 | tf_op jit(solution)/shard_map/add | solution.py:127
  104.8 2.3 %gather_fusion.9 = f32[256,32]{1,0:T(8,128)S(1)} fusion(f32[32,4096]{0,1:T(8,128)} %copy.197, s32[1024]{0:T(1024)S(1)} %pad_clamp_fusion.1), kind=kCustom, calls=%fused_computation.9 | custom fusion | bytes 66560 | tf_op jit(solution)/shard_map/gather | solution.py:108
  107.2 4.1 %collective-permute-start.6 = (bf16[32,1024]{1,0:T(8,128)(2,1)S(1)}, bf16[32,1024]{1,0:T(8,128)(2,1)S(1)}, u32[]{:S(2)}, u32[]{:S(2)}) collective-permute-start(bf16[32,1024]{1,0:T(8,128)(2,1)S(1)} %get-tuple-element.20), channel_id=1, source_target_pairs={{0,4},{4,8},{8,12},{12,16},{16,20},{20,24},{24,28},{1,5},{5,9},{9,... | collective-permute-start | bytes 196616 | tf_op jit(solution)/shard_map/ppermute | solution.py:22
  111.3 1.3 collective-permute-start.7
  112.6 4.0 %collective-permute-done.8 = f32[32,256]{0,1:T(8,128)S(1)} collective-permute-done((f32[32,256]{0,1:T(8,128)S(1)}, f32[32,256]{0,1:T(8,128)S(1)}, u32[]{:S(2)}, u32[]{:S(2)}) %collective-permute-start.8) | collective-permute-done | bytes 32800 | tf_op jit(solution)/shard_map/ppermute | solution.py:35
  116.6 0.7 gather_fusion.10
  117.5 5.4 %all_gather.11 = f32[128,256]{1,0:T(8,128)S(1)} all-gather(f32[32,256]{1,0:T(8,128)S(1)} %copy.198), channel_id=1, replica_groups=mesh['comp'=8,'harm'=4] {'harm'}, dimensions={0}, use_global_device_ids=true | all-gather | bytes 163840 | tf_op jit(solution)/shard_map/all_gather | solution.py:111
  122.9 2.9 %fusion.3 = f32[1024,256]{1,0:T(8,128)S(1)} fusion(f32[128,256]{1,0:T(8,128)S(1)} %all_gather.11, f32[256]{0:T(256)S(1)} %bitcast.200, f32[256]{0:T(256)S(1)} %bitcast.203, pred[256]{0:T(512)(128)(4,1)S(1)} %copy-done.44, s32[128]{0:T(128)S(1)} %copy-done.32, pred[128]{0:T(512)(128)(4,1)S(1)} %copy-done.37), kind=kOutput, calls=%fused_computation.18 | convolution fusion | flops 405667840 | bytes 1182592 | tf_op jit(solution)/shard_map/dot_general | solution.py:112
  125.9 1.1 fusion.12
  127.1 2.3 %scatter_custom_fusion.2 = f32[32,4096]{0,1:T(8,128)S(1)} fusion(s32[256]{0:T(256)} %bitcast.196, f32[256,32]{1,0:T(8,128)S(1)} %copy.199, f32[]{:T(128)} %constant.58.clone.1), kind=kCustom, calls=%fused_computation.41 | custom fusion | flops 8192 | bytes 524800 | tf_op jit(solution)/shard_map/scatter-add | solution.py:125
  129.5 1.4 copy.200
  130.9 0.6 copy-done.23
  131.5 0.9 copy_bitcast_fusion
  132.4 1.0 gather_fusion.8
  133.4 6.2 %convolution_bitcast_fusion = f32[32,4,8,128]{3,2,1,0:T(8,128)S(1)} fusion(bf16[32,32,8,128]{3,0,2,1:T(8,128)(2,1)S(1)} %bitcast.174, bf16[32,8,128,128]{3,2,1,0:T(8,128)(2,1)} %param.12), kind=kOutput, calls=%fused_computation.29 | convolution fusion | flops 268435456 | bytes 11010048 | tf_op jit(solution)/shard_map/rsij,hrsj->hri/dot_general | solution.py:103
  139.7 6.3 %convolution_bitcast_fusion.1 = f32[32,4,8,128]{3,2,1,0:T(8,128)S(1)} fusion(bf16[32,32,8,128]{3,0,2,1:T(8,128)(2,1)S(1)} %bitcast.175, bf16[32,8,128,128]{3,2,1,0:T(8,128)(2,1)} %param.11), kind=kOutput, calls=%fused_computation.30 | convolution fusion | flops 268435456 | bytes 11010048 | tf_op jit(solution)/shard_map/rsij,hrsj->hri/dot_general | solution.py:100
  146.0 1.2 divide_add_fusion
  (124 shorter events, 1.2 us)
Async XLA Ops:
  0.6 1.2 slice-start.1
  0.7 11.9 %copy-start.30 = (s32[128]{0:T(128)}, s32[128]{0:T(128)S(1)}, u32[]{:S(2)}) copy-start(s32[128]{0:T(128)S(1)} %iota_select_fusion) | copy-start | bytes 1540
  5.2 2.0 %slice-start = ((bf16[32,8,128,128]{3,2,1,0:T(8,128)(2,1)}), bf16[32,1,128,128]{3,2,1,0:T(8,128)(2,1)S(1)}, s32[]{:S(2)}) async-start(bf16[32,8,128,128]{3,2,1,0:T(8,128)(2,1)} %param.12), calls=%async_computation | async-start | bytes 2097152 | tf_op jit(solution)/shard_map/slice | solution.py:82
  7.2 5.5 %copy-start.14 = (f32[32,128]{1,0:T(8,128)}, f32[32,128]{1,0:T(8,128)S(1)}, u32[]{:S(2)}) copy-start(f32[32,128]{1,0:T(8,128)S(1)} %copy.176) | copy-start | bytes 49156
  7.2 5.5 %copy-start = (f32[32,4096]{1,0:T(8,128)S(1)}, f32[32,4096]{1,0:T(8,128)}, u32[]{:S(2)}) copy-start(f32[32,4096]{1,0:T(8,128)} %param.10) | copy-start | bytes 1572868
  12.5 1.3 copy-start.33
  12.6 0.6 copy-start.18
  12.7 12.0 %copy-start.34 = (s32[1,256]{1,0:T(1,128)S(1)}, s32[1,256]{1,0:T(1,128)}, u32[]{:S(2)}) copy-start(s32[1,256]{1,0:T(1,128)} %param.15) | copy-start | bytes 3076
  13.2 15.9 %copy-start.7 = (bf16[32,4096]{1,0:T(8,128)(2,1)}, bf16[32,4096]{1,0:T(8,128)(2,1)S(1)}, u32[]{:S(2)}) copy-start(bf16[32,4096]{1,0:T(8,128)(2,1)S(1)} %get-tuple-element.18) | copy-start | bytes 786436
  13.2 14.9 %copy-start.29 = (s32[32,8]{0,1:T(8,128)S(1)}, s32[32,8]{0,1:T(8,128)}, u32[]{:S(2)}) copy-start(s32[32,8]{0,1:T(8,128)} %param.13) | copy-start | bytes 3076
  13.8 0.5 copy-start.28
  15.1 13.3 %collective-permute-start.2 = (f32[32,256]{0,1:T(8,128)S(1)}, f32[32,256]{0,1:T(8,128)S(1)}, u32[]{:S(2)}, u32[]{:S(2)}) collective-permute-start(f32[32,256]{0,1:T(8,128)S(1)} %bitcast.190), channel_id=1, source_target_pairs={{0,16},{16,0},{4,20},{20,4},{8,24},{24,8},{12,28},{28,12},{1,17},{... | collective-permute-start | bytes 98312 | tf_op jit(solution)/shard_map/ppermute | solution.py:35
  19.9 23.3 %collective-permute-start = (bf16[32,1024]{1,0:T(8,128)(2,1)}, bf16[32,1024]{1,0:T(8,128)(2,1)S(1)}, u32[]{:S(2)}, u32[]{:S(2)}) collective-permute-start(bf16[32,1024]{1,0:T(8,128)(2,1)} %get-tuple-element.24), channel_id=1, source_target_pairs={{0,4},{4,8},{8,12},{12,16},{16,20},{20,24},{24,28},{1,5},{5,9},{9,... | collective-permute-start | bytes 196616 | tf_op jit(solution)/shard_map/ppermute | solution.py:22
  23.3 20.5 %collective-permute-start.1 = (bf16[32,1024]{1,0:T(8,128)(2,1)}, bf16[32,1024]{1,0:T(8,128)(2,1)}, u32[]{:S(2)}, u32[]{:S(2)}) collective-permute-start(bf16[32,1024]{1,0:T(8,128)(2,1)} %get-tuple-element.25), channel_id=1, source_target_pairs={{4,0},{8,4},{12,8},{16,12},{20,16},{24,20},{28,24},{5,1},{9,5},{13... | collective-permute-start | bytes 196616 | tf_op jit(solution)/shard_map/ppermute | solution.py:23
  24.6 13.7 %copy-start.35 = (pred[128]{0:T(512)(128)(4,1)}, pred[128]{0:T(512)(128)(4,1)S(1)}, u32[]{:S(2)}) copy-start(pred[128]{0:T(512)(128)(4,1)S(1)} %iota_compare_fusion.1) | copy-start | bytes 388
  28.3 10.0 %copy-start.42 = (pred[256]{0:T(512)(128)(4,1)}, pred[256]{0:T(512)(128)(4,1)S(1)}, u32[]{:S(2)}) copy-start(pred[256]{0:T(512)(128)(4,1)S(1)} %iota_compare_fusion) | copy-start | bytes 772
  28.4 9.9 %copy-start.25 = (f32[32]{0:T(128)}, f32[32]{0:T(128)S(1)}, u32[]{:S(2)}) copy-start(f32[32]{0:T(128)S(1)} %dynamic_slice.13) | copy-start | bytes 388
  43.2 0.6 copy-start.22
  52.0 6.3 %copy-start.8 = (bf16[32,4096]{1,0:T(8,128)(2,1)S(1)}, bf16[32,4096]{1,0:T(8,128)(2,1)}, u32[]{:S(2)}) copy-start(bf16[32,4096]{1,0:T(8,128)(2,1)} %copy-done.7) | copy-start | bytes 786436
  52.0 6.3 %copy-start.13 = (f32[32,4096]{1,0:T(8,128)S(1)}, f32[32,4096]{1,0:T(8,128)}, u32[]{:S(2)}) copy-start(f32[32,4096]{1,0:T(8,128)} %copy.186) | copy-start | bytes 1572868
  52.1 6.3 %copy-start.15 = (f32[32,128]{1,0:T(8,128)S(1)}, f32[32,128]{1,0:T(8,128)}, u32[]{:S(2)}) copy-start(f32[32,128]{1,0:T(8,128)} %copy-done.14) | copy-start | bytes 49156
  52.1 6.3 %copy-start.19 = (f32[32,128]{1,0:T(8,128)S(1)}, f32[32,128]{1,0:T(8,128)}, u32[]{:S(2)}) copy-start(f32[32,128]{1,0:T(8,128)} %copy-done.18) | copy-start | bytes 49156
  58.7 20.5 %copy-start.3 = (f32[32,4096]{1,0:T(8,128)}, f32[32,4096]{1,0:T(8,128)S(1)}, u32[]{:S(2)}) copy-start(f32[32,4096]{1,0:T(8,128)S(1)} %get-tuple-element.17) | copy-start | bytes 1572868
  58.8 20.5 %copy-start.9 = (bf16[32,4096]{1,0:T(8,128)(2,1)}, bf16[32,4096]{1,0:T(8,128)(2,1)S(1)}, u32[]{:S(2)}) copy-start(bf16[32,4096]{1,0:T(8,128)(2,1)S(1)} %get-tuple-element.16) | copy-start | bytes 786436
  58.8 20.5 %copy-start.31 = (s32[128]{0:T(128)S(1)}, s32[128]{0:T(128)}, u32[]{:S(2)}) copy-start(s32[128]{0:T(128)} %copy-done.30) | copy-start | bytes 1540
  58.8 20.5 %copy-start.36 = (pred[128]{0:T(512)(128)(4,1)S(1)}, pred[128]{0:T(512)(128)(4,1)}, u32[]{:S(2)}) copy-start(pred[128]{0:T(512)(128)(4,1)} %copy-done.35) | copy-start | bytes 388
  58.8 20.5 %copy-start.38 = (f32[1,256]{1,0:T(1,128)S(1)}, f32[1,256]{1,0:T(1,128)}, u32[]{:S(2)}) copy-start(f32[1,256]{1,0:T(1,128)} %param.18) | copy-start | bytes 3076
  58.8 20.5 %copy-start.40 = (f32[1,256]{1,0:T(1,128)S(1)}, f32[1,256]{1,0:T(1,128)}, u32[]{:S(2)}) copy-start(f32[1,256]{1,0:T(1,128)} %param.17) | copy-start | bytes 3076
  58.8 20.5 %copy-start.43 = (pred[256]{0:T(512)(128)(4,1)S(1)}, pred[256]{0:T(512)(128)(4,1)}, u32[]{:S(2)}) copy-start(pred[256]{0:T(512)(128)(4,1)} %copy-done.42) | copy-start | bytes 772
  63.1 10.0 %collective-permute-start.5 = (f32[32,256]{0,1:T(8,128)S(1)}, f32[32,256]{0,1:T(8,128)S(1)}, u32[]{:S(2)}, u32[]{:S(2)}) collective-permute-start(f32[32,256]{0,1:T(8,128)S(1)} %bitcast.192), channel_id=1, source_target_pairs={{0,16},{16,0},{4,20},{20,4},{8,24},{24,8},{12,28},{28,12},{1,17},{... | collective-permute-start | bytes 98312 | tf_op jit(solution)/shard_map/ppermute | solution.py:35
  66.3 21.0 %collective-permute-start.3 = (bf16[32,1024]{1,0:T(8,128)(2,1)S(1)}, bf16[32,1024]{1,0:T(8,128)(2,1)S(1)}, u32[]{:S(2)}, u32[]{:S(2)}) collective-permute-start(bf16[32,1024]{1,0:T(8,128)(2,1)S(1)} %get-tuple-element.22), channel_id=1, source_target_pairs={{0,4},{4,8},{8,12},{12,16},{16,20},{20,24},{24,28},{1,5},{5,9},{9,... | collective-permute-start | bytes 196616 | tf_op jit(solution)/shard_map/ppermute | solution.py:22
  68.0 19.8 %collective-permute-start.4 = (bf16[32,1024]{1,0:T(8,128)(2,1)S(1)}, bf16[32,1024]{1,0:T(8,128)(2,1)}, u32[]{:S(2)}, u32[]{:S(2)}) collective-permute-start(bf16[32,1024]{1,0:T(8,128)(2,1)S(1)} %get-tuple-element.23), channel_id=1, source_target_pairs={{4,0},{8,4},{12,8},{16,12},{20,16},{24,20},{28,24},{5,1},{9,5},{13... | collective-permute-start | bytes 196616 | tf_op jit(solution)/shard_map/ppermute | solution.py:23
  79.3 3.0 %copy-start.26 = (f32[32]{0:T(128)S(1)}, f32[32]{0:T(128)}, u32[]{:S(2)}) copy-start(f32[32]{0:T(128)} %copy-done.25) | copy-start | bytes 388
  87.2 0.6 copy-start.24
  96.1 6.3 %copy-start.4 = (f32[32,4096]{1,0:T(8,128)S(1)}, f32[32,4096]{1,0:T(8,128)}, u32[]{:S(2)}) copy-start(f32[32,4096]{1,0:T(8,128)} %copy-done.3) | copy-start | bytes 1572868
  96.1 6.3 %copy-start.10 = (bf16[32,4096]{1,0:T(8,128)(2,1)S(1)}, bf16[32,4096]{1,0:T(8,128)(2,1)}, u32[]{:S(2)}) copy-start(bf16[32,4096]{1,0:T(8,128)(2,1)} %copy-done.9) | copy-start | bytes 786436
  96.1 6.3 %copy-start.12 = (f32[32,4096]{1,0:T(8,128)S(1)}, f32[32,4096]{1,0:T(8,128)}, u32[]{:S(2)}) copy-start(f32[32,4096]{1,0:T(8,128)} %copy.193) | copy-start | bytes 1572868
  96.1 6.3 %copy-start.16 = (f32[32,128]{1,0:T(8,128)S(1)}, f32[32,128]{1,0:T(8,128)}, u32[]{:S(2)}) copy-start(f32[32,128]{1,0:T(8,128)} %copy-done.14) | copy-start | bytes 49156
  96.1 6.3 %copy-start.20 = (f32[32,128]{1,0:T(8,128)S(1)}, f32[32,128]{1,0:T(8,128)}, u32[]{:S(2)}) copy-start(f32[32,128]{1,0:T(8,128)} %copy-done.18) | copy-start | bytes 49156
  102.8 20.1 %copy-start.1 = (f32[32,4096]{1,0:T(8,128)}, f32[32,4096]{1,0:T(8,128)S(1)}, u32[]{:S(2)}) copy-start(f32[32,4096]{1,0:T(8,128)S(1)} %get-tuple-element.15) | copy-start | bytes 1572868
  102.8 20.1 %copy-start.5 = (bf16[32,4096]{1,0:T(8,128)(2,1)}, bf16[32,4096]{1,0:T(8,128)(2,1)S(1)}, u32[]{:S(2)}) copy-start(bf16[32,4096]{1,0:T(8,128)(2,1)S(1)} %get-tuple-element.14) | copy-start | bytes 786436
  102.8 20.1 %copy-start.32 = (s32[128]{0:T(128)S(1)}, s32[128]{0:T(128)}, u32[]{:S(2)}) copy-start(s32[128]{0:T(128)} %copy-done.30) | copy-start | bytes 1540
  102.8 20.1 %copy-start.37 = (pred[128]{0:T(512)(128)(4,1)S(1)}, pred[128]{0:T(512)(128)(4,1)}, u32[]{:S(2)}) copy-start(pred[128]{0:T(512)(128)(4,1)} %copy-done.35) | copy-start | bytes 388
  102.8 20.1 %copy-start.39 = (f32[1,256]{1,0:T(1,128)S(1)}, f32[1,256]{1,0:T(1,128)}, u32[]{:S(2)}) copy-start(f32[1,256]{1,0:T(1,128)} %param.18) | copy-start | bytes 3076
  102.8 20.1 %copy-start.41 = (f32[1,256]{1,0:T(1,128)S(1)}, f32[1,256]{1,0:T(1,128)}, u32[]{:S(2)}) copy-start(f32[1,256]{1,0:T(1,128)} %param.17) | copy-start | bytes 3076
  102.8 20.1 %copy-start.44 = (pred[256]{0:T(512)(128)(4,1)S(1)}, pred[256]{0:T(512)(128)(4,1)}, u32[]{:S(2)}) copy-start(pred[256]{0:T(512)(128)(4,1)} %copy-done.42) | copy-start | bytes 772
  107.1 9.5 %collective-permute-start.8 = (f32[32,256]{0,1:T(8,128)S(1)}, f32[32,256]{0,1:T(8,128)S(1)}, u32[]{:S(2)}, u32[]{:S(2)}) collective-permute-start(f32[32,256]{0,1:T(8,128)S(1)} %bitcast.191), channel_id=1, source_target_pairs={{0,16},{16,0},{4,20},{20,4},{8,24},{24,8},{12,28},{28,12},{1,17},{... | collective-permute-start | bytes 98312 | tf_op jit(solution)/shard_map/ppermute | solution.py:35
  107.2 23.6 %collective-permute-start.6 = (bf16[32,1024]{1,0:T(8,128)(2,1)S(1)}, bf16[32,1024]{1,0:T(8,128)(2,1)S(1)}, u32[]{:S(2)}, u32[]{:S(2)}) collective-permute-start(bf16[32,1024]{1,0:T(8,128)(2,1)S(1)} %get-tuple-element.20), channel_id=1, source_target_pairs={{0,4},{4,8},{8,12},{12,16},{16,20},{20,24},{24,28},{1,5},{5,9},{9,... | collective-permute-start | bytes 196616 | tf_op jit(solution)/shard_map/ppermute | solution.py:22
  111.3 20.2 %collective-permute-start.7 = (bf16[32,1024]{1,0:T(8,128)(2,1)S(1)}, bf16[32,1024]{1,0:T(8,128)(2,1)}, u32[]{:S(2)}, u32[]{:S(2)}) collective-permute-start(bf16[32,1024]{1,0:T(8,128)(2,1)S(1)} %get-tuple-element.21), channel_id=1, source_target_pairs={{4,0},{8,4},{12,8},{16,12},{20,16},{24,20},{28,24},{5,1},{9,5},{13... | collective-permute-start | bytes 196616 | tf_op jit(solution)/shard_map/ppermute | solution.py:23
  122.9 3.0 %copy-start.27 = (f32[32]{0:T(128)S(1)}, f32[32]{0:T(128)}, u32[]{:S(2)}) copy-start(f32[32]{0:T(128)} %copy-done.25) | copy-start | bytes 388
  127.1 4.4 %copy-start.6 = (bf16[32,4096]{1,0:T(8,128)(2,1)S(1)}, bf16[32,4096]{1,0:T(8,128)(2,1)}, u32[]{:S(2)}) copy-start(bf16[32,4096]{1,0:T(8,128)(2,1)} %copy-done.5) | copy-start | bytes 786436
  130.8 0.6 copy-start.23
  139.6 6.3 %copy-start.2 = (f32[32,4096]{1,0:T(8,128)S(1)}, f32[32,4096]{1,0:T(8,128)}, u32[]{:S(2)}) copy-start(f32[32,4096]{1,0:T(8,128)} %copy-done.1) | copy-start | bytes 1572868
  139.6 6.3 %copy-start.11 = (f32[32,4096]{1,0:T(8,128)S(1)}, f32[32,4096]{1,0:T(8,128)}, u32[]{:S(2)}) copy-start(f32[32,4096]{1,0:T(8,128)} %copy.200) | copy-start | bytes 1572868
  139.6 6.3 %copy-start.17 = (f32[32,128]{1,0:T(8,128)S(1)}, f32[32,128]{1,0:T(8,128)}, u32[]{:S(2)}) copy-start(f32[32,128]{1,0:T(8,128)} %copy-done.14) | copy-start | bytes 49156
  139.6 6.3 %copy-start.21 = (f32[32,128]{1,0:T(8,128)S(1)}, f32[32,128]{1,0:T(8,128)}, u32[]{:S(2)}) copy-start(f32[32,128]{1,0:T(8,128)} %copy-done.18) | copy-start | bytes 49156
where the time goes:
time: 148 us; the launch traced here: 147 us
  matrix products  50.3 us (34%)
  local copies, waits for them, and re-layouts  34.7 us (23%)
  starting transfers between devices  20.5 us (14%)
  blocking collectives  16.2 us (11%)
  other arithmetic  15 us (10%)
  waiting for transfers between devices  7.77 us (5%)
  between operations  2.81 us (2%)
    dot_general x3, matrix products, local(): jnp.einsum('rsij,hrsj->hri', stiff_blocks, picked, preferred_element_type...  18.8 us
    dot_general x3, matrix products, local(): jnp.einsum('rsij,hrsj->hri', mass_blocks, picked, preferred_element_type=...  18.5 us
    all_gather x3, blocking collectives, local(): gathered = lax.all_gather(relative, 'harm', axis=0, tiled=True)  16.2 us
    unnamed x92, local copies, waits for them, and re-layouts  9.63 us
    dot_general x3, matrix products, local(): jnp.dot(instant_table, gathered, precision=lax.Precision.HIGHEST)  9.52 us
    ppermute x3, starting transfers between devices, with_halo(): before = lax.ppermute(last, axis, up)  9.28 us
    ppermute x3, waiting for transfers between devices, swapped(): return lax.ppermute(block, axis, route)  7.75 us
    ppermute x3, starting transfers between devices, swapped(): return lax.ppermute(block, axis, route)  7.36 us
  transfers between devices with their start and end apart: 9, of which 2 were waited for; matrix products, arithmetic and copies ran while one was open for 21% of the time, Pallas kernels for 0%

commit v1 on v0

v1 whole, which is shorter than its diff:
```python
import functools
import math

import jax
import jax.numpy as jnp
import numpy as np
from jax import lax
from jax.experimental import pallas as pl
from jax.experimental.pallas import tpu as pltpu
from jax.sharding import PartitionSpec as P

H = 128
TIME_POINTS = 1024
BAND = 8
ITERS = 3
MESH = pl.DeviceIdType.MESH
F32 = jnp.float32
BF16 = jnp.bfloat16
NN = (((1,), (0,)), ((), ()))
NT = (((1,), (1,)), ((), ()))


def host_tables(harm_parts):
    column = np.arange(H)
    orders = np.where(column <= H // 2, column, column - H // 2)
    phase = np.arange(TIME_POINTS)[:, None] * orders[None, :] % TIME_POINTS
    angle = phase * (2.0 * math.pi / TIME_POINTS)
    table = np.where(column[None, :] <= H // 2, np.cos(angle), np.sin(angle))
    table = table.astype(np.float32)
    high = table.astype(BF16)
    low = (table - high.astype(np.float32)).astype(BF16)
    to_time = np.concatenate([high, low], axis=1)
    back = np.stack(
        [high.T.reshape(harm_parts, -1, TIME_POINTS), low.T.reshape(harm_parts, -1, TIME_POINTS)], axis=1
    )
    return to_time, back.reshape(harm_parts, -1, TIME_POINTS)


def halves(value):
    high = value.astype(BF16)
    low = (value - high.astype(F32)).astype(BF16)
    return high, low


def stacked(value):
    return jnp.concatenate(halves(value), axis=0)


def folded(value):
    half = value.shape[0] // 2
    return value[:half] + value[half:]


def product(left, right, dims):
    return lax.dot_general(left, right, dims, preferred_element_type=F32)


def kernel(
    comp_size,
    harm_size,
    load_ref,
    stiff_hbm,
    mass_hbm,
    cols_ref,
    rows_ref,
    partner_ref,
    count_ref,
    normal_ref,
    spring_ref,
    freq_ref,
    time_ref,
    back_ref,
    disp_out,
    res_out,
    stiff_ref,
    mass_ref,
    field,
    shift,
    dyn_ref,
    hot,
    perm,
    ext,
    halo,
    swap_out,
    swap_in,
    shared,
    rel_high,
    rel_low,
    diag_sem,
    block_sem,
    halo_send,
    halo_recv,
    swap_send,
    swap_recv,
    share_send,
    share_recv,
):
    comp = lax.axis_index("comp")
    harm = lax.axis_index("harm")
    block_rows = stiff_ref.shape[0]
    slots = stiff_ref.shape[1]
    blk = stiff_ref.shape[2]
    nh = load_ref.shape[0]
    wide = 2 * blk
    pairs = block_rows // 2
    chunks = block_rows // BAND
    cmax = rows_ref.shape[1]
    first_row = comp * block_rows
    has_prev = comp > 0
    has_next = comp < comp_size - 1
    after = lax.rem(comp + 1, comp_size)
    before = lax.rem(comp + comp_size - 1, comp_size)
    facing = lax.rem(comp + comp_size // 2, comp_size)
    order = list(range(1, chunks - 1)) + [0, chunks - 1]

    diag_copies = [
        pltpu.make_async_copy(source.at[:, pl.ds(0, 1)], held.at[:, pl.ds(0, 1)], diag_sem.at[i])
        for i, (source, held) in enumerate(((stiff_hbm, stiff_ref), (mass_hbm, mass_ref)))
    ]
    for copy in diag_copies:
        copy.start()
    block_copies = {}
    for c in order:
        span = (pl.ds(c * BAND, BAND), pl.ds(1, slots - 1))
        block_copies[c] = [
            pltpu.make_async_copy(source.at[span], held.at[span], block_sem.at[c, i])
            for i, (source, held) in enumerate(((stiff_hbm, stiff_ref), (mass_hbm, mass_ref)))
        ]
        for copy in block_copies[c]:
            copy.start()

    barrier = pltpu.get_barrier_semaphore()
    pl.semaphore_signal(barrier, inc=1, device_id=(facing, harm), device_id_type=MESH)
    for step in range(1, harm_size):
        peer = lax.rem(harm + step, harm_size)
        pl.semaphore_signal(barrier, inc=1, device_id=(comp, peer), device_id_type=MESH)

    @pl.when(has_prev)
    def _():
        pl.semaphore_signal(barrier, inc=1, device_id=(before, harm), device_id_type=MESH)

    @pl.when(has_next)
    def _():
        pl.semaphore_signal(barrier, inc=1, device_id=(after, harm), device_id_type=MESH)

    row_list = rows_ref[...]
    sub = lax.broadcasted_iota(jnp.int32, (wide, cmax), 0)

    def mark(p, carry):
        base = pl.multiple_of(p * wide, wide)
        hot[pl.ds(base, wide), :] = jnp.where(sub == row_list - base, 1.0, 0.0).astype(BF16)
        return carry

    lax.fori_loop(0, pairs, mark, 0)
    slot_axis = lax.broadcasted_iota(jnp.int32, (cmax, cmax), 0)
    perm[...] = jnp.where(slot_axis == partner_ref[...], 1.0, 0.0).astype(BF16)
    ext[pl.ds(0, BAND)] = jnp.zeros((BAND, nh, blk), BF16)
    ext[pl.ds(BAND + block_rows, BAND)] = jnp.zeros((BAND, nh, blk), BF16)

    def factor_of(width):
        index = harm * nh + lax.broadcasted_iota(jnp.int32, (nh, width), 0)
        wave = jnp.where(index <= H // 2, index, index - H // 2).astype(F32)
        value = freq_ref[0] * wave * (2.0 / H)
        return value * value

    slot_index = lax.broadcasted_iota(jnp.int32, (1, cmax), 1)
    slot_scale = jnp.where(slot_index < count_ref[0], normal_ref[...], 0.0)
    own_index = harm * nh + lax.broadcasted_iota(jnp.int32, (nh, cmax), 0)
    own_weight = jnp.where(own_index == 0, 1.0 / TIME_POINTS, 2.0 / TIME_POINTS)
    spring_ratio = spring_ref[...] / normal_ref[...]

    for copy in diag_copies:
        copy.wait()
    eye = lax.broadcasted_iota(jnp.int32, (blk, blk), 0) == lax.broadcasted_iota(
        jnp.int32, (blk, blk), 1
    )

    def diagonal(ref, p):
        parts = [
            jnp.sum(jnp.where(eye, ref[2 * p + q, 0].astype(F32), 0.0), axis=0, keepdims=True)
            for q in range(2)
        ]
        return jnp.concatenate(parts, axis=1)

    def put_rounded(p, value):
        rounded = value.astype(BF16)
        for q in range(2):
            ext[BAND + 2 * p + q] = rounded[:, q * blk : (q + 1) * blk]

    def lanes(p):
        return pl.ds(pl.multiple_of(p * wide, wide), wide)

    def start_field(p, listed):
        dynamic = diagonal(stiff_ref, p) - factor_of(wide) * diagonal(mass_ref, p)
        value = load_ref[:, lanes(p)] / dynamic
        dyn_ref[p] = dynamic
        field[p] = value
        put_rounded(p, value)
        return listed + product(stacked(value), hot[lanes(p), :], NN)

    listed = lax.fori_loop(0, pairs, start_field, jnp.zeros((2 * nh, cmax), F32))

    neighbours = jnp.minimum(comp, 1) + jnp.minimum(comp_size - 1 - comp, 1)
    pl.semaphore_wait(barrier, harm_size + neighbours)

    def apply_rows(chunk):
        def body(p, carry):
            applied = []
            for q in range(2):
                r = 2 * p + q
                picked = jnp.concatenate(
                    [
                        ext[jnp.clip(cols_ref[r, s] - first_row + BAND, 0, ext.shape[0] - 1)]
                        for s in range(slots)
                    ],
                    axis=1,
                )
                blocks = jnp.concatenate(
                    [
                        jnp.concatenate([ref[r, s] for s in range(slots)], axis=1)
                        for ref in (stiff_ref, mass_ref)
                    ],
                    axis=0,
                )
                both = product(picked, blocks, NT)
                applied.append(both[:, :blk] - factor_of(blk) * both[:, blk:])
            rounded = jnp.concatenate([ext[BAND + 2 * p + q] for q in range(2)], axis=1)
            gap = field[p] - rounded.astype(F32)
            shift[p] = (
                load_ref[:, lanes(p)] - jnp.concatenate(applied, axis=1) - dyn_ref[p] * gap
            )
            return carry

        lax.fori_loop(chunk * BAND // 2, (chunk + 1) * BAND // 2, body, 0)

    for k in range(ITERS):
        up = pltpu.make_async_remote_copy(
            src_ref=ext.at[pl.ds(block_rows, BAND)],
            dst_ref=halo.at[k, 0],
            send_sem=halo_send.at[k, 0],
            recv_sem=halo_recv.at[k, 0],
            device_id=(after, harm),
            device_id_type=MESH,
        )
        down = pltpu.make_async_remote_copy(
            src_ref=ext.at[pl.ds(BAND, BAND)],
            dst_ref=halo.at[k, 1],
            send_sem=halo_send.at[k, 1],
            recv_sem=halo_recv.at[k, 1],
            device_id=(before, harm),
            device_id_type=MESH,
        )
        own = folded(listed)
        swap_out[k] = own
        swap = pltpu.make_async_remote_copy(
            src_ref=swap_out.at[k],
            dst_ref=swap_in.at[k],
            send_sem=swap_send.at[k],
            recv_sem=swap_recv.at[k],
            device_id=(facing, harm),
            device_id_type=MESH,
        )
        swap.start()

        @pl.when(has_next)
        def _():
            up.start()

        @pl.when(has_prev)
        def _():
            down.start()

        def ready(chunk):
            if k == 0:
                for copy in block_copies[chunk]:
                    copy.wait()

        ready(order[0])
        apply_rows(order[0])

        swap.wait()
        mirrored = folded(product(stacked(swap_in[k]), perm[...], NN))
        shared[k, harm] = (swap_out[k] - mirrored) * spring_ratio
        sends = []
        for step in range(1, harm_size):
            sends.append(
                pltpu.make_async_remote_copy(
                    src_ref=shared.at[k, harm],
                    dst_ref=shared.at[k, harm],
                    send_sem=share_send.at[k, step - 1],
                    recv_sem=share_recv.at[k, step - 1],
                    device_id=(comp, lax.rem(harm + step, harm_size)),
                    device_id_type=MESH,
                )
            )
            sends[-1].start()

        for chunk in order[1:-2]:
            ready(chunk)
            apply_rows(chunk)

        @pl.when(has_next)
        def _():
            up.wait_send()
            down.wait_recv()
            ext[pl.ds(BAND + block_rows, BAND)] = halo[k, 1]

        @pl.when(has_prev)
        def _():
            down.wait_send()
            up.wait_recv()
            ext[pl.ds(0, BAND)] = halo[k, 0]

        for chunk in order[-2:]:
            ready(chunk)
            apply_rows(chunk)

        for send in sends:
            send.wait()
        for part in range(harm_size):
            high, low = halves(shared[k, part])
            for copy in range(2):
                rel_high[pl.ds(copy * H + part * nh, nh), :] = high
                rel_low[pl.ds(copy * H + part * nh, nh), :] = low
        total = jnp.zeros((2 * nh, cmax), F32)
        extra = jnp.zeros((nh, cmax), F32)
        step_points = 2 * H
        for t in range(0, TIME_POINTS, step_points):
            rows_now = time_ref[pl.ds(t, step_points), :]
            values = product(rows_now, rel_high[...], NN) + product(rows_now, rel_low[...], NN)
            high, low = halves(jnp.tanh(values))
            back = back_ref[harm, :, pl.ds(t, step_points)]
            total = total + product(back, high, NN)
            extra = extra + product(back[:nh], low, NN)
        projected = stacked((folded(total) + extra) * own_weight * slot_scale)

        last = k == ITERS - 1

        def finish(p, carry):
            nonlinear = folded(product(projected, hot[lanes(p), :], NT))
            residual = shift[p] - nonlinear
            value = field[p] + residual / dyn_ref[p]
            if last:
                disp_out[:, lanes(p)] = value
                res_out[:, lanes(p)] = residual
                return carry
            field[p] = value
            put_rounded(p, value)
            return carry + product(stacked(value), hot[lanes(p), :], NN)

        listed = lax.fori_loop(
            0, pairs, finish, jnp.zeros((8, 128) if last else (2 * nh, cmax), F32)
        )


def local(comp_size, harm_size, *arrays):
    load, stiff_blocks, mass_blocks = arrays[:3]
    nh, dofs = load.shape
    block_rows, slots, blk, _ = stiff_blocks.shape
    cmax = arrays[4].shape[1]
    to_time, back = host_tables(harm_size)
    vmem = pl.BlockSpec(memory_space=pltpu.VMEM)
    smem = pl.BlockSpec(memory_space=pltpu.SMEM)
    hbm = pl.BlockSpec(memory_space=pl.ANY)
    wide = (block_rows // 2, nh, 2 * blk)
    dma = pltpu.SemaphoreType.DMA
    return pl.pallas_call(
        functools.partial(kernel, comp_size, harm_size),
        out_shape=(jax.ShapeDtypeStruct((nh, dofs), F32),) * 2,
        in_specs=[vmem, hbm, hbm, smem, vmem, vmem, smem, vmem, vmem, smem, vmem, vmem],
        out_specs=(vmem, vmem),
        scratch_shapes=[
            pltpu.VMEM(stiff_blocks.shape, BF16),
            pltpu.VMEM(mass_blocks.shape, BF16),
            pltpu.VMEM(wide, F32),
            pltpu.VMEM(wide, F32),
            pltpu.VMEM(wide, F32),
            pltpu.VMEM((dofs, cmax), BF16),
            pltpu.VMEM((cmax, cmax), BF16),
            pltpu.VMEM((block_rows + 2 * BAND, nh, blk), BF16),
            pltpu.VMEM((ITERS, 2, BAND, nh, blk), BF16),
            pltpu.VMEM((ITERS, nh, cmax), F32),
            pltpu.VMEM((ITERS, nh, cmax), F32),
            pltpu.VMEM((ITERS, harm_size, nh, cmax), F32),
            pltpu.VMEM((2 * H, cmax), BF16),
            pltpu.VMEM((2 * H, cmax), BF16),
            dma((2,)),
            dma((block_rows // BAND, 2)),
            dma((ITERS, 2)),
            dma((ITERS, 2)),
            dma((ITERS,)),
            dma((ITERS,)),
            dma((ITERS, harm_size - 1)),
            dma((ITERS, harm_size - 1)),
        ],
        compiler_params=pltpu.CompilerParams(
            collective_id=0, has_side_effects=True, vmem_limit_bytes=56 * 1024 * 1024
        ),
    )(*arrays, jnp.asarray(to_time), jnp.asarray(back))


def solution(mesh):
    placed = (
        P("harm", "comp"),
        P("comp", None, None, None),
        P("comp", None, None, None),
        P("comp", None),
        P("comp", None),
        P("comp", None),
        P("comp"),
        P("comp", None),
        P("comp", None),
        P(),
    )
    return jax.shard_map(
        functools.partial(local, mesh.shape["comp"], mesh.shape["harm"]),
        mesh=mesh,
        in_specs=placed,
        out_specs=(P("harm", "comp"), P("harm", "comp")),
        check_vma=False,
    )
```

time: 148 us -> 59.7 us (0.40)
  Pallas kernels: 0 us -> 52.4 us
  matrix products: 50.3 us -> 0 us
  local copies, waits for them, and re-layouts: 34.7 us -> 5.1 us
  starting transfers between devices: 20.5 us -> 0 us
  blocking collectives: 16.2 us -> 0 us
  other arithmetic: 15 us -> 0 us
  waiting for transfers between devices: 7.77 us -> 0 us
    pallas_call x0 -> x1, Pallas kernels: none -> 52.4 us  [local(): pl.pallas_call(functools.partial(kernel, comp_size, harm_size), out_shape...]
    dot_general x12 -> x0, matrix products: 50.3 us -> none  [the longest x3 18.8 us: local(): jnp.einsum('rsij,hrsj->hri', stiff_blocks, picked, preferred_element_type...]
    ppermute x9 -> x0, starting transfers between devices: 20.5 us -> none  [the longest x3 9.28 us: with_halo(): before = lax.ppermute(last, axis, up)]
    all_gather x3 -> x0, blocking collectives: 16.2 us -> none  [local(): gathered = lax.all_gather(relative, 'harm', axis=0, tiled=True)]
    gather x11 -> x0, local copies, waits for them, and re-layouts: 14.4 us -> none  [the longest x3 5.35 us: local(): listed = displacement[:, slot_rows]]
    ppermute x9 -> x0, waiting for transfers between devices: 7.77 us -> none  [the longest x3 7.75 us: swapped(): return lax.ppermute(block, axis, route)]
    scatter-add x3 -> x0, other arithmetic: 6.87 us -> none  [local(): jnp.zeros_like(displacement).at[:, slot_rows].add(own_force)]
    unnamed x92 -> x3, local copies, waits for them, and re-layouts: 9.63 us -> 5.1 us
  transfers between devices with their start and end apart: 9 -> 0, of which waited for: 2 -> 0; matrix products, arithmetic and copies ran while one was open for 21% -> 0% of each run, Pallas kernels for 0% -> 0%
where the time goes in v1:
time: 59.7 us; the launch traced here: 59.4 us
  Pallas kernels  52.4 us (88%)
  local copies, waits for them, and re-layouts  5.1 us (9%)
  between operations  1.93 us (3%)
    pallas_call x1, Pallas kernels, local(): pl.pallas_call(functools.partial(kernel, comp_size, harm_size), out_shape...  52.4 us
    unnamed x3, local copies, waits for them, and re-layouts  5.1 us

profile of v1, /device:TPU:0, one launch (start us, length us, event | category | flops | bytes accessed | tf_op | source)
XLA Modules:
  0.0 59.4 jit_solution(1130417324043571433)
XLA Ops:
  1.9 1.4 %copy.14.cols_ref = s32[32,8]{1,0:T(8,128)} copy(s32[32,8]{0,1:T(8,128)} %param.15) | data formatting | bytes 2048 | tf_op args[3]
  3.3 52.4 %shard_map.131 = (f32[32,4096]{1,0:T(8,128)}, f32[32,4096]{1,0:T(8,128)}) custom-call(f32[32,4096]{1,0:T(8,128)} %load_ref.1, bf16[32,8,128,128]{3,2,1,0:T(8,128)(2,1)} %stiff_hbm.1, bf16[32,8,128,128]{3,2,1,0:T(8,128)(2,1)} %mass_hbm.1, s32[32,8]{1,0:T(8,128)} %copy.14.cols_ref, s32[1,256]{1,0:T(1,128)} %rows_ref.1, s32[1,256]{1,0:T(1,128)} %partner_ref.1, ...), custom_call_target="tpu_custom_call" | custom-call | tf_op jit(solution)/shard_map/pallas_call | solution.py:367
  55.7 1.9 %copy.19 = f32[32,4096]{1,0:T(8,128)} copy(f32[32,4096]{1,0:T(8,128)} %get-tuple-element.4) | data formatting | bytes 1048576
  57.5 1.9 %copy.20 = f32[32,4096]{1,0:T(8,128)} copy(f32[32,4096]{1,0:T(8,128)} %get-tuple-element.5) | data formatting | bytes 1048576

commit v2 on v1

--- a/solution.py
+++ b/solution.py
@@ -58,7 +58,7 @@
 def kernel(
     comp_size,
     harm_size,
-    load_ref,
+    load_hbm,
     stiff_hbm,
     mass_hbm,
     cols_ref,
@@ -68,15 +68,20 @@
     normal_ref,
     spring_ref,
     freq_ref,
+    time_hbm,
+    back_hbm,
+    disp_out,
+    res_out,
+    load_ref,
     time_ref,
     back_ref,
-    disp_out,
-    res_out,
     stiff_ref,
     mass_ref,
     field,
     shift,
     dyn_ref,
+    inv_ref,
+    slot_inverse,
     hot,
     perm,
     ext,
@@ -86,6 +91,7 @@
     shared,
     rel_high,
     rel_low,
+    side_sem,
     diag_sem,
     block_sem,
     halo_send,
@@ -119,6 +125,13 @@
     ]
     for copy in diag_copies:
         copy.start()
+    load_copy, *table_copies = [
+        pltpu.make_async_copy(source, held, side_sem.at[i])
+        for i, (source, held) in enumerate(
+            ((load_hbm, load_ref), (time_hbm, time_ref), (back_hbm, back_ref))
+        )
+    ]
+    load_copy.start()
     block_copies = {}
     for c in order:
         span = (pl.ds(c * BAND, BAND), pl.ds(1, slots - 1))
@@ -128,6 +141,8 @@
         ]
         for copy in block_copies[c]:
             copy.start()
+    for copy in table_copies:
+        copy.start()
 
     barrier = pltpu.get_barrier_semaphore()
     pl.semaphore_signal(barrier, inc=1, device_id=(facing, harm), device_id_type=MESH)
@@ -171,6 +186,7 @@
 
     for copy in diag_copies:
         copy.wait()
+    load_copy.wait()
     eye = lax.broadcasted_iota(jnp.int32, (blk, blk), 0) == lax.broadcasted_iota(
         jnp.int32, (blk, blk), 1
     )
@@ -190,27 +206,40 @@
     def lanes(p):
         return pl.ds(pl.multiple_of(p * wide, wide), wide)
 
-    def start_field(p, listed):
-        dynamic = diagonal(stiff_ref, p) - factor_of(wide) * diagonal(mass_ref, p)
+    def start_field(p, gathered):
+        stiff_diag = diagonal(stiff_ref, p)
+        mass_diag = diagonal(mass_ref, p)
+        dynamic = stiff_diag - factor_of(wide) * mass_diag
         value = load_ref[:, lanes(p)] / dynamic
         dyn_ref[p] = dynamic
+        inv_ref[p] = 1.0 / dynamic
         field[p] = value
         put_rounded(p, value)
-        return listed + product(stacked(value), hot[lanes(p), :], NN)
-
-    listed = lax.fori_loop(0, pairs, start_field, jnp.zeros((2 * nh, cmax), F32))
+        high, low = halves(value)
+        diagonals = jnp.concatenate(
+            [jnp.broadcast_to(part, (8, wide)) for part in (stiff_diag, mass_diag)], axis=0
+        )
+        left = jnp.concatenate([high, low, diagonals.astype(BF16)], axis=0)
+        return gathered + product(left, hot[lanes(p), :], NN)
+
+    gathered = lax.fori_loop(
+        0, pairs, start_field, jnp.zeros((2 * nh + 16, cmax), F32), unroll=2
+    )
+    listed = folded(gathered[: 2 * nh])
+    slot_dynamic = gathered[2 * nh : 2 * nh + 1] - factor_of(cmax) * gathered[2 * nh + 8 : 2 * nh + 9]
+    slot_inverse[...] = 1.0 / slot_dynamic
 
     neighbours = jnp.minimum(comp, 1) + jnp.minimum(comp_size - 1 - comp, 1)
     pl.semaphore_wait(barrier, harm_size + neighbours)
 
-    def apply_rows(chunk):
+    def apply_rows(first, stop, gathered):
         def body(p, carry):
             applied = []
             for q in range(2):
                 r = 2 * p + q
                 picked = jnp.concatenate(
                     [
-                        ext[jnp.clip(cols_ref[r, s] - first_row + BAND, 0, ext.shape[0] - 1)]
+                        ext[jnp.clip(cols_ref[s, r] - first_row + BAND, 0, ext.shape[0] - 1)]
                         for s in range(slots)
                     ],
                     axis=1,
@@ -226,12 +255,26 @@
                 applied.append(both[:, :blk] - factor_of(blk) * both[:, blk:])
             rounded = jnp.concatenate([ext[BAND + 2 * p + q] for q in range(2)], axis=1)
             gap = field[p] - rounded.astype(F32)
-            shift[p] = (
-                load_ref[:, lanes(p)] - jnp.concatenate(applied, axis=1) - dyn_ref[p] * gap
-            )
-            return carry
-
-        lax.fori_loop(chunk * BAND // 2, (chunk + 1) * BAND // 2, body, 0)
+            value = load_ref[:, lanes(p)] - jnp.concatenate(applied, axis=1) - dyn_ref[p] * gap
+            shift[p] = value
+            if carry is None:
+                return carry
+            return carry + product(stacked(value), hot[lanes(p), :], NN)
+
+        return lax.fori_loop(first * BAND // 2, stop * BAND // 2, body, gathered, unroll=2)
+
+    def swap_copy(k):
+        return pltpu.make_async_remote_copy(
+            src_ref=swap_out.at[k],
+            dst_ref=swap_in.at[k],
+            send_sem=swap_send.at[k],
+            recv_sem=swap_recv.at[k],
+            device_id=(facing, harm),
+            device_id_type=MESH,
+        )
+
+    swap_out[0] = listed
+    swap_copy(0).start()
 
     for k in range(ITERS):
         up = pltpu.make_async_remote_copy(
@@ -250,18 +293,6 @@
             device_id=(before, harm),
             device_id_type=MESH,
         )
-        own = folded(listed)
-        swap_out[k] = own
-        swap = pltpu.make_async_remote_copy(
-            src_ref=swap_out.at[k],
-            dst_ref=swap_in.at[k],
-            send_sem=swap_send.at[k],
-            recv_sem=swap_recv.at[k],
-            device_id=(facing, harm),
-            device_id_type=MESH,
-        )
-        swap.start()
-
         @pl.when(has_next)
         def _():
             up.start()
@@ -270,15 +301,21 @@
         def _():
             down.start()
 
-        def ready(chunk):
-            if k == 0:
+        last = k == ITERS - 1
+
+        def span(first, stop, gathered):
+            if k > 0:
+                return apply_rows(first, stop, gathered)
+            for chunk in range(first, stop):
                 for copy in block_copies[chunk]:
                     copy.wait()
-
-        ready(order[0])
-        apply_rows(order[0])
-
-        swap.wait()
+                gathered = apply_rows(chunk, chunk + 1, gathered)
+            return gathered
+
+        gathered = None if last else jnp.zeros((2 * nh, cmax), F32)
+        gathered = span(1, chunks - 1, gathered)
+
+        swap_copy(k).wait()
         mirrored = folded(product(stacked(swap_in[k]), perm[...], NN))
         shared[k, harm] = (swap_out[k] - mirrored) * spring_ratio
         sends = []
@@ -295,10 +332,6 @@
             )
             sends[-1].start()
 
-        for chunk in order[1:-2]:
-            ready(chunk)
-            apply_rows(chunk)
-
         @pl.when(has_next)
         def _():
             up.wait_send()
@@ -311,10 +344,12 @@
             up.wait_recv()
             ext[pl.ds(0, BAND)] = halo[k, 0]
 
-        for chunk in order[-2:]:
-            ready(chunk)
-            apply_rows(chunk)
-
+        gathered = span(0, 1, gathered)
+        gathered = span(chunks - 1, chunks, gathered)
+
+        if k == 0:
+            for copy in table_copies:
+                copy.wait()
         for send in sends:
             send.wait()
         for part in range(harm_size):
@@ -332,29 +367,29 @@
             back = back_ref[harm, :, pl.ds(t, step_points)]
             total = total + product(back, high, NN)
             extra = extra + product(back[:nh], low, NN)
-        projected = stacked((folded(total) + extra) * own_weight * slot_scale)
-
-        last = k == ITERS - 1
+        force = (folded(total) + extra) * own_weight * slot_scale
+        projected = stacked(force)
+        if not last:
+            swap_out[k + 1] = swap_out[k] + (folded(gathered) - force) * slot_inverse[...]
+            swap_copy(k + 1).start()
 
         def finish(p, carry):
             nonlinear = folded(product(projected, hot[lanes(p), :], NT))
             residual = shift[p] - nonlinear
-            value = field[p] + residual / dyn_ref[p]
+            value = field[p] + residual * inv_ref[p]
             if last:
                 disp_out[:, lanes(p)] = value
                 res_out[:, lanes(p)] = residual
-                return carry
-            field[p] = value
-            put_rounded(p, value)
-            return carry + product(stacked(value), hot[lanes(p), :], NN)
-
-        listed = lax.fori_loop(
-            0, pairs, finish, jnp.zeros((8, 128) if last else (2 * nh, cmax), F32)
-        )
+            else:
+                field[p] = value
+                put_rounded(p, value)
+            return carry
+
+        lax.fori_loop(0, pairs, finish, 0, unroll=4)
 
 
 def local(comp_size, harm_size, *arrays):
-    load, stiff_blocks, mass_blocks = arrays[:3]
+    load, stiff_blocks, mass_blocks, block_cols = arrays[:4]
     nh, dofs = load.shape
     block_rows, slots, blk, _ = stiff_blocks.shape
     cmax = arrays[4].shape[1]
@@ -367,14 +402,19 @@
     return pl.pallas_call(
         functools.partial(kernel, comp_size, harm_size),
         out_shape=(jax.ShapeDtypeStruct((nh, dofs), F32),) * 2,
-        in_specs=[vmem, hbm, hbm, smem, vmem, vmem, smem, vmem, vmem, smem, vmem, vmem],
+        in_specs=[hbm, hbm, hbm, smem, vmem, vmem, smem, vmem, vmem, smem, hbm, hbm],
         out_specs=(vmem, vmem),
         scratch_shapes=[
+            pltpu.VMEM(load.shape, F32),
+            pltpu.VMEM(to_time.shape, BF16),
+            pltpu.VMEM(back.shape, BF16),
             pltpu.VMEM(stiff_blocks.shape, BF16),
             pltpu.VMEM(mass_blocks.shape, BF16),
             pltpu.VMEM(wide, F32),
             pltpu.VMEM(wide, F32),
             pltpu.VMEM(wide, F32),
+            pltpu.VMEM(wide, F32),
+            pltpu.VMEM((nh, cmax), F32),
             pltpu.VMEM((dofs, cmax), BF16),
             pltpu.VMEM((cmax, cmax), BF16),
             pltpu.VMEM((block_rows + 2 * BAND, nh, blk), BF16),
@@ -384,6 +424,7 @@
             pltpu.VMEM((ITERS, harm_size, nh, cmax), F32),
             pltpu.VMEM((2 * H, cmax), BF16),
             pltpu.VMEM((2 * H, cmax), BF16),
+            dma((3,)),
             dma((2,)),
             dma((block_rows // BAND, 2)),
             dma((ITERS, 2)),
@@ -394,9 +435,9 @@
             dma((ITERS, harm_size - 1)),
         ],
         compiler_params=pltpu.CompilerParams(
-            collective_id=0, has_side_effects=True, vmem_limit_bytes=56 * 1024 * 1024
+            collective_id=0, has_side_effects=True, vmem_limit_bytes=52 * 1024 * 1024
         ),
-    )(*arrays, jnp.asarray(to_time), jnp.asarray(back))
+    )(load, stiff_blocks, mass_blocks, block_cols.T, *arrays[4:], jnp.asarray(to_time), jnp.asarray(back))
 
 
 def solution(mesh):

time: 59.7 us -> 44.6 us (0.75)
  Pallas kernels: 52.4 us -> 36.4 us
  local copies, waits for them, and re-layouts: 5.1 us -> 6.02 us
    pallas_call x1, Pallas kernels: 52.4 us -> 36.4 us  [local(): pl.pallas_call(functools.partial(kernel, comp_size, harm_size), out_shape...]
    unnamed x3 -> x14, local copies, waits for them, and re-layouts: 5.1 us -> 6.02 us
where the time goes in v2:
time: 44.6 us; the launch traced here: 44.3 us
  Pallas kernels  36.4 us (82%)
  local copies, waits for them, and re-layouts  6.02 us (13%)
  between operations  1.95 us (4%)
    pallas_call x1, Pallas kernels, local(): pl.pallas_call(functools.partial(kernel, comp_size, harm_size), out_shape...  36.4 us
    unnamed x14, local copies, waits for them, and re-layouts  6.02 us

profile of v2, /device:TPU:0, one launch (start us, length us, event | category | flops | bytes accessed | tf_op | source)
XLA Modules:
  0.0 44.3 jit_solution(4623144082106048517)
XLA Ops:
  1.9 0.0 copy-start
  1.9 1.0 %copy-done = f32[32,4096]{1,0:T(8,128)S(1)} copy-done((f32[32,4096]{1,0:T(8,128)S(1)}, f32[32,4096]{1,0:T(8,128)}, u32[]{:S(2)}) %copy-start) | copy-done | bytes 524312
  3.0 0.0 copy-start.1
  3.0 0.7 %copy-done.1 = s32[32,8]{0,1:T(8,128)S(1)} copy-done((s32[32,8]{0,1:T(8,128)S(1)}, s32[32,8]{0,1:T(8,128)}, u32[]{:S(2)}) %copy-start.1) | copy-done | bytes 1048
  3.7 0.0 copy-start.2
  3.7 0.7 %copy-done.2 = s32[1,256]{1,0:T(1,128)S(1)} copy-done((s32[1,256]{1,0:T(1,128)S(1)}, s32[1,256]{1,0:T(1,128)}, u32[]{:S(2)}) %copy-start.2) | copy-done | bytes 1048
  4.3 0.0 copy-start.3
  4.3 0.7 %copy-done.3 = s32[1,256]{1,0:T(1,128)S(1)} copy-done((s32[1,256]{1,0:T(1,128)S(1)}, s32[1,256]{1,0:T(1,128)}, u32[]{:S(2)}) %copy-start.3) | copy-done | bytes 1048
  5.0 0.0 copy-start.4
  5.0 0.7 %copy-done.4 = f32[1,256]{1,0:T(1,128)S(1)} copy-done((f32[1,256]{1,0:T(1,128)S(1)}, f32[1,256]{1,0:T(1,128)}, u32[]{:S(2)}) %copy-start.4) | copy-done | bytes 1048
  5.7 0.0 copy-start.5
  5.7 0.7 %copy-done.5 = f32[1,256]{1,0:T(1,128)S(1)} copy-done((f32[1,256]{1,0:T(1,128)S(1)}, f32[1,256]{1,0:T(1,128)}, u32[]{:S(2)}) %copy-start.5) | copy-done | bytes 1048
  6.4 36.4 %shard_map.131 = (f32[32,4096]{1,0:T(8,128)S(1)}, f32[32,4096]{1,0:T(8,128)S(1)}) custom-call(f32[32,4096]{1,0:T(8,128)S(1)} %copy-done, bf16[32,8,128,128]{3,2,1,0:T(8,128)(2,1)} %stiff_hbm.1, bf16[32,8,128,128]{3,2,1,0:T(8,128)(2,1)} %mass_hbm.1, s32[8,32]{1,0:T(8,128)S(1)} %bitcast.1, s32[1,256]{1,0:T(1,128)S(1)} %copy-done.2, s32[1,256]{1,0:T(1,128)S(1)} %copy-done.3, ...), custom_call_target="tpu_custom_call" | custom-call | tf_op jit(solution)/shard_map/pallas_call | solution.py:402
  42.7 0.8 %copy.18 = f32[32,4096]{1,0:T(8,128)} copy(f32[32,4096]{1,0:T(8,128)S(1)} %get-tuple-element.4) | data formatting | bytes 1048576
  43.5 0.8 %copy.19 = f32[32,4096]{1,0:T(8,128)} copy(f32[32,4096]{1,0:T(8,128)S(1)} %get-tuple-element.5) | data formatting | bytes 1048576
Async XLA Ops:
  1.9 1.0 %copy-start = (f32[32,4096]{1,0:T(8,128)S(1)}, f32[32,4096]{1,0:T(8,128)}, u32[]{:S(2)}) copy-start(f32[32,4096]{1,0:T(8,128)} %load_hbm.1) | copy-start | bytes 1572868
  3.0 0.7 %copy-start.1 = (s32[32,8]{0,1:T(8,128)S(1)}, s32[32,8]{0,1:T(8,128)}, u32[]{:S(2)}) copy-start(s32[32,8]{0,1:T(8,128)} %param.15) | copy-start | bytes 3076
  3.7 0.7 %copy-start.2 = (s32[1,256]{1,0:T(1,128)S(1)}, s32[1,256]{1,0:T(1,128)}, u32[]{:S(2)}) copy-start(s32[1,256]{1,0:T(1,128)} %rows_ref.1) | copy-start | bytes 3076
  4.3 0.7 %copy-start.3 = (s32[1,256]{1,0:T(1,128)S(1)}, s32[1,256]{1,0:T(1,128)}, u32[]{:S(2)}) copy-start(s32[1,256]{1,0:T(1,128)} %partner_ref.1) | copy-start | bytes 3076
  5.0 0.7 %copy-start.4 = (f32[1,256]{1,0:T(1,128)S(1)}, f32[1,256]{1,0:T(1,128)}, u32[]{:S(2)}) copy-start(f32[1,256]{1,0:T(1,128)} %normal_ref.1) | copy-start | bytes 3076
  5.7 0.7 %copy-start.5 = (f32[1,256]{1,0:T(1,128)S(1)}, f32[1,256]{1,0:T(1,128)}, u32[]{:S(2)}) copy-start(f32[1,256]{1,0:T(1,128)} %spring_ref.1) | copy-start | bytes 3076

commit v3 on v2

--- a/solution.py
+++ b/solution.py
@@ -61,17 +61,23 @@
     load_hbm,
     stiff_hbm,
     mass_hbm,
-    cols_ref,
-    rows_ref,
-    partner_ref,
+    cols_hbm,
+    rows_hbm,
+    partner_hbm,
     count_ref,
-    normal_ref,
-    spring_ref,
+    normal_hbm,
+    spring_hbm,
     freq_ref,
     time_hbm,
     back_hbm,
     disp_out,
     res_out,
+    cols_ref,
+    rows_ref,
+    partner_ref,
+    normal_ref,
+    spring_ref,
+    factor_ref,
     load_ref,
     time_ref,
     back_ref,
@@ -91,6 +97,7 @@
     shared,
     rel_high,
     rel_low,
+    small_sem,
     side_sem,
     diag_sem,
     block_sem,
@@ -119,6 +126,20 @@
     facing = lax.rem(comp + comp_size // 2, comp_size)
     order = list(range(1, chunks - 1)) + [0, chunks - 1]
 
+    small_copies = [
+        pltpu.make_async_copy(source, held, small_sem.at[i])
+        for i, (source, held) in enumerate(
+            (
+                (rows_hbm, rows_ref),
+                (partner_hbm, partner_ref),
+                (normal_hbm, normal_ref),
+                (spring_hbm, spring_ref),
+                (cols_hbm, cols_ref),
+            )
+        )
+    ]
+    for copy in small_copies:
+        copy.start()
     diag_copies = [
         pltpu.make_async_copy(source.at[:, pl.ds(0, 1)], held.at[:, pl.ds(0, 1)], diag_sem.at[i])
         for i, (source, held) in enumerate(((stiff_hbm, stiff_ref), (mass_hbm, mass_ref)))
@@ -158,6 +179,9 @@
     def _():
         pl.semaphore_signal(barrier, inc=1, device_id=(after, harm), device_id_type=MESH)
 
+    for copy in small_copies:
+        copy.wait()
+
     row_list = rows_ref[...]
     sub = lax.broadcasted_iota(jnp.int32, (wide, cmax), 0)
 
@@ -166,7 +190,7 @@
         hot[pl.ds(base, wide), :] = jnp.where(sub == row_list - base, 1.0, 0.0).astype(BF16)
         return carry
 
-    lax.fori_loop(0, pairs, mark, 0)
+    lax.fori_loop(0, pairs, mark, 0, unroll=2)
     slot_axis = lax.broadcasted_iota(jnp.int32, (cmax, cmax), 0)
     perm[...] = jnp.where(slot_axis == partner_ref[...], 1.0, 0.0).astype(BF16)
     ext[pl.ds(0, BAND)] = jnp.zeros((BAND, nh, blk), BF16)
@@ -178,6 +202,7 @@
         value = freq_ref[0] * wave * (2.0 / H)
         return value * value
 
+    factor_ref[...] = factor_of(wide)
     slot_index = lax.broadcasted_iota(jnp.int32, (1, cmax), 1)
     slot_scale = jnp.where(slot_index < count_ref[0], normal_ref[...], 0.0)
     own_index = harm * nh + lax.broadcasted_iota(jnp.int32, (nh, cmax), 0)
@@ -209,10 +234,11 @@
     def start_field(p, gathered):
         stiff_diag = diagonal(stiff_ref, p)
         mass_diag = diagonal(mass_ref, p)
-        dynamic = stiff_diag - factor_of(wide) * mass_diag
-        value = load_ref[:, lanes(p)] / dynamic
+        dynamic = stiff_diag - factor_ref[...] * mass_diag
+        inverse = 1.0 / dynamic
+        value = load_ref[:, lanes(p)] * inverse
         dyn_ref[p] = dynamic
-        inv_ref[p] = 1.0 / dynamic
+        inv_ref[p] = inverse
         field[p] = value
         put_rounded(p, value)
         high, low = halves(value)
@@ -223,7 +249,7 @@
         return gathered + product(left, hot[lanes(p), :], NN)
 
     gathered = lax.fori_loop(
-        0, pairs, start_field, jnp.zeros((2 * nh + 16, cmax), F32), unroll=2
+        0, pairs, start_field, jnp.zeros((2 * nh + 16, cmax), F32), unroll=4
     )
     listed = folded(gathered[: 2 * nh])
     slot_dynamic = gathered[2 * nh : 2 * nh + 1] - factor_of(cmax) * gathered[2 * nh + 8 : 2 * nh + 9]
@@ -252,7 +278,7 @@
                     axis=0,
                 )
                 both = product(picked, blocks, NT)
-                applied.append(both[:, :blk] - factor_of(blk) * both[:, blk:])
+                applied.append(both[:, :blk] - factor_ref[:, :blk] * both[:, blk:])
             rounded = jnp.concatenate([ext[BAND + 2 * p + q] for q in range(2)], axis=1)
             gap = field[p] - rounded.astype(F32)
             value = load_ref[:, lanes(p)] - jnp.concatenate(applied, axis=1) - dyn_ref[p] * gap
@@ -261,7 +287,7 @@
                 return carry
             return carry + product(stacked(value), hot[lanes(p), :], NN)
 
-        return lax.fori_loop(first * BAND // 2, stop * BAND // 2, body, gathered, unroll=2)
+        return lax.fori_loop(first * BAND // 2, stop * BAND // 2, body, gathered, unroll=4)
 
     def swap_copy(k):
         return pltpu.make_async_remote_copy(
@@ -273,10 +299,7 @@
             device_id_type=MESH,
         )
 
-    swap_out[0] = listed
-    swap_copy(0).start()
-
-    for k in range(ITERS):
+    def halo_copies(k):
         up = pltpu.make_async_remote_copy(
             src_ref=ext.at[pl.ds(block_rows, BAND)],
             dst_ref=halo.at[k, 0],
@@ -293,6 +316,11 @@
             device_id=(before, harm),
             device_id_type=MESH,
         )
+        return up, down
+
+    def start_halo(k):
+        up, down = halo_copies(k)
+
         @pl.when(has_next)
         def _():
             up.start()
@@ -301,6 +329,12 @@
         def _():
             down.start()
 
+    swap_out[0] = listed
+    swap_copy(0).start()
+    start_halo(0)
+
+    for k in range(ITERS):
+        up, down = halo_copies(k)
         last = k == ITERS - 1
 
         def span(first, stop, gathered):
@@ -385,7 +419,12 @@
                 put_rounded(p, value)
             return carry
 
-        lax.fori_loop(0, pairs, finish, 0, unroll=4)
+        edge = BAND // 2
+        lax.fori_loop(0, edge, finish, 0, unroll=edge)
+        lax.fori_loop(pairs - edge, pairs, finish, 0, unroll=edge)
+        if not last:
+            start_halo(k + 1)
+        lax.fori_loop(edge, pairs - edge, finish, 0, unroll=8)
 
 
 def local(comp_size, harm_size, *arrays):
@@ -396,15 +435,21 @@
     to_time, back = host_tables(harm_size)
     vmem = pl.BlockSpec(memory_space=pltpu.VMEM)
     smem = pl.BlockSpec(memory_space=pltpu.SMEM)
-    hbm = pl.BlockSpec(memory_space=pl.ANY)
+    hbm = pl.BlockSpec(memory_space=pltpu.HBM)
     wide = (block_rows // 2, nh, 2 * blk)
     dma = pltpu.SemaphoreType.DMA
     return pl.pallas_call(
         functools.partial(kernel, comp_size, harm_size),
         out_shape=(jax.ShapeDtypeStruct((nh, dofs), F32),) * 2,
-        in_specs=[hbm, hbm, hbm, smem, vmem, vmem, smem, vmem, vmem, smem, hbm, hbm],
+        in_specs=[hbm, hbm, hbm, hbm, hbm, hbm, smem, hbm, hbm, smem, hbm, hbm],
         out_specs=(vmem, vmem),
         scratch_shapes=[
+            pltpu.SMEM((slots, block_rows), jnp.int32),
+            pltpu.VMEM((1, cmax), jnp.int32),
+            pltpu.VMEM((1, cmax), jnp.int32),
+            pltpu.VMEM((1, cmax), F32),
+            pltpu.VMEM((1, cmax), F32),
+            pltpu.VMEM((nh, 2 * blk), F32),
             pltpu.VMEM(load.shape, F32),
             pltpu.VMEM(to_time.shape, BF16),
             pltpu.VMEM(back.shape, BF16),
@@ -424,6 +469,7 @@
             pltpu.VMEM((ITERS, harm_size, nh, cmax), F32),
             pltpu.VMEM((2 * H, cmax), BF16),
             pltpu.VMEM((2 * H, cmax), BF16),
+            dma((5,)),
             dma((3,)),
             dma((2,)),
             dma((block_rows // BAND, 2)),

time: 44.6 us -> 40.9 us (0.917)
  Pallas kernels: 36.4 us -> 32.7 us
    pallas_call x1, Pallas kernels: 36.4 us -> 32.7 us  [local(): pl.pallas_call(functools.partial(kernel, comp_size, harm_size), out_shape...]
where the time goes in v3:
time: 40.9 us; the launch traced here: 40.6 us
  Pallas kernels  32.7 us (80%)
  local copies, waits for them, and re-layouts  6.02 us (15%)
  between operations  1.95 us (5%)
    pallas_call x1, Pallas kernels, local(): pl.pallas_call(functools.partial(kernel, comp_size, harm_size), out_shape...  32.7 us
    unnamed x14, local copies, waits for them, and re-layouts  6.02 us

profile of v3, /device:TPU:0, one launch (start us, length us, event | category | flops | bytes accessed | tf_op | source)
XLA Modules:
  0.0 40.6 jit_solution(7610599008430736598)
XLA Ops:
  1.9 0.0 copy-start
  1.9 1.0 %copy-done = f32[32,4096]{1,0:T(8,128)S(1)} copy-done((f32[32,4096]{1,0:T(8,128)S(1)}, f32[32,4096]{1,0:T(8,128)}, u32[]{:S(2)}) %copy-start) | copy-done | bytes 524312
  3.0 0.0 copy-start.1
  3.0 0.7 %copy-done.1 = s32[32,8]{0,1:T(8,128)S(1)} copy-done((s32[32,8]{0,1:T(8,128)S(1)}, s32[32,8]{0,1:T(8,128)}, u32[]{:S(2)}) %copy-start.1) | copy-done | bytes 1048
  3.7 0.0 copy-start.2
  3.7 0.7 %copy-done.2 = s32[1,256]{1,0:T(1,128)S(1)} copy-done((s32[1,256]{1,0:T(1,128)S(1)}, s32[1,256]{1,0:T(1,128)}, u32[]{:S(2)}) %copy-start.2) | copy-done | bytes 1048
  4.3 0.0 copy-start.3
  4.3 0.7 %copy-done.3 = s32[1,256]{1,0:T(1,128)S(1)} copy-done((s32[1,256]{1,0:T(1,128)S(1)}, s32[1,256]{1,0:T(1,128)}, u32[]{:S(2)}) %copy-start.3) | copy-done | bytes 1048
  5.0 0.0 copy-start.4
  5.0 0.7 %copy-done.4 = f32[1,256]{1,0:T(1,128)S(1)} copy-done((f32[1,256]{1,0:T(1,128)S(1)}, f32[1,256]{1,0:T(1,128)}, u32[]{:S(2)}) %copy-start.4) | copy-done | bytes 1048
  5.7 0.0 copy-start.5
  5.7 0.7 %copy-done.5 = f32[1,256]{1,0:T(1,128)S(1)} copy-done((f32[1,256]{1,0:T(1,128)S(1)}, f32[1,256]{1,0:T(1,128)}, u32[]{:S(2)}) %copy-start.5) | copy-done | bytes 1048
  6.4 32.7 %shard_map.131 = (f32[32,4096]{1,0:T(8,128)S(1)}, f32[32,4096]{1,0:T(8,128)S(1)}) custom-call(f32[32,4096]{1,0:T(8,128)S(1)} %copy-done, bf16[32,8,128,128]{3,2,1,0:T(8,128)(2,1)} %stiff_hbm.1, bf16[32,8,128,128]{3,2,1,0:T(8,128)(2,1)} %mass_hbm.1, s32[8,32]{1,0:T(8,128)S(1)} %bitcast.1, s32[1,256]{1,0:T(1,128)S(1)} %copy-done.2, s32[1,256]{1,0:T(1,128)S(1)} %copy-done.3, ...), custom_call_target="tpu_custom_call" | custom-call | tf_op jit(solution)/shard_map/pallas_call | solution.py:441
  39.0 0.8 %copy.18 = f32[32,4096]{1,0:T(8,128)} copy(f32[32,4096]{1,0:T(8,128)S(1)} %get-tuple-element.4) | data formatting | bytes 1048576
  39.8 0.8 %copy.19 = f32[32,4096]{1,0:T(8,128)} copy(f32[32,4096]{1,0:T(8,128)S(1)} %get-tuple-element.5) | data formatting | bytes 1048576
Async XLA Ops:
  1.9 1.0 %copy-start = (f32[32,4096]{1,0:T(8,128)S(1)}, f32[32,4096]{1,0:T(8,128)}, u32[]{:S(2)}) copy-start(f32[32,4096]{1,0:T(8,128)} %load_hbm.1) | copy-start | bytes 1572868
  3.0 0.7 %copy-start.1 = (s32[32,8]{0,1:T(8,128)S(1)}, s32[32,8]{0,1:T(8,128)}, u32[]{:S(2)}) copy-start(s32[32,8]{0,1:T(8,128)} %param.15) | copy-start | bytes 3076
  3.7 0.7 %copy-start.2 = (s32[1,256]{1,0:T(1,128)S(1)}, s32[1,256]{1,0:T(1,128)}, u32[]{:S(2)}) copy-start(s32[1,256]{1,0:T(1,128)} %rows_hbm.1) | copy-start | bytes 3076
  4.3 0.7 %copy-start.3 = (s32[1,256]{1,0:T(1,128)S(1)}, s32[1,256]{1,0:T(1,128)}, u32[]{:S(2)}) copy-start(s32[1,256]{1,0:T(1,128)} %partner_hbm.1) | copy-start | bytes 3076
  5.0 0.7 %copy-start.4 = (f32[1,256]{1,0:T(1,128)S(1)}, f32[1,256]{1,0:T(1,128)}, u32[]{:S(2)}) copy-start(f32[1,256]{1,0:T(1,128)} %normal_hbm.1) | copy-start | bytes 3076
  5.7 0.7 %copy-start.5 = (f32[1,256]{1,0:T(1,128)S(1)}, f32[1,256]{1,0:T(1,128)}, u32[]{:S(2)}) copy-start(f32[1,256]{1,0:T(1,128)} %spring_hbm.1) | copy-start | bytes 3076
